TPU v7x, 128 devices: a whole 4x4x4 slice. The times are simulated.
128 devices in a mesh: ctx: 32 (over x, y, core), tp: 4 (over z).
Axes of the slice: x: 4, y: 4, z: 4, core: 2. Of those that a mesh axis runs over, the one named last changes fastest.
Arguments:
- attention: bfloat16 [16384, 2048], P('ctx', 'tp'), may hold values from -6 to 6
- residual: bfloat16 [16384, 2048], P(('ctx', 'tp')), may hold values from -6 to 6
- w_out: bfloat16 [2048, 2048], P('tp'), may hold values from -0.125 to 0.125
- w_qkv: bfloat16 [3072, 2048], P('tp'), may hold values from -0.125 to 0.125
- norm_moe: float32 [2048], replicated, may hold values from 0.25 to 1.75
- norm_attn: float32 [2048], replicated, may hold values from 0.25 to 1.75
- expert_ids: int32 [16384, 4], P(('ctx', 'tp')), may hold values from 0 to 63, all different within a row; in each aligned block of 128 rows (0 to 127, 128 to 255, ...) at most 12 rows name the same one
- expert_gates: float32 [16384, 4], P(('ctx', 'tp')), may hold values from 0.02 to 0.3
- w_gate: bfloat16 [128, 2048, 384], P(('ctx', 'tp')), may hold values from -0.125 to 0.125
- w_up: bfloat16 [128, 2048, 384], P(('ctx', 'tp')), may hold values from -0.125 to 0.125
- w_down: bfloat16 [128, 384, 2048], P(('ctx', 'tp')), may hold values from -0.21875 to 0.21875
- d_projected: bfloat16 [16384, 3072], P('ctx', 'tp'), may hold values from -6 to 6
- d_stream: bfloat16 [16384, 2048], P(('ctx', 'tp')), may hold values from -6 to 6
Outputs:
- projected: bfloat16 [16384, 3072], P('ctx', 'tp')
- stream: bfloat16 [16384, 2048], P(('ctx', 'tp'))
- grad_attention: bfloat16 [16384, 2048], P('ctx', 'tp')
- grad_residual: bfloat16 [16384, 2048], P(('ctx', 'tp'))
- grad_w_out: bfloat16 [2048, 2048], P('tp', 'ctx')
- grad_w_gate: bfloat16 [128, 2048, 384], P(('ctx', 'tp'))
- grad_w_up: bfloat16 [128, 2048, 384], P(('ctx', 'tp'))
- grad_w_down: bfloat16 [128, 384, 2048], P(('ctx', 'tp'))
Inputs may be any that keep to these rules, and one draw needn't show every extreme that they name: `expert_ids`: each row names 4 different experts. Among the rows of one device no expert is named more than 12 times, a bound that some block reaches there.
All inputs are finite; a program needn't handle non-finite values.
Results may differ from a plain program's by a relative error of at most 0.0075.
Values may be sent and summed in bfloat16 or wider, within the bound.
No kernel may reach another device: no remote copies, remote signals or barrier semaphores. Data moves between devices by JAX's collectives and lax.ppermute only.
A program may use at most 128 MiB of HBM per device.

v0:
```python
import jax
import jax.numpy as jnp
from jax import lax
from jax.sharding import PartitionSpec as P

EPSILON = 1e-06


def swapped(block, axis, bit):
    count = lax.axis_size(axis)
    route = []
    for low in range(count):
        high = low | 1 << bit
        if high != low and high < count:
            route += [(low, high), (high, low)]
    return lax.ppermute(block, axis, route)


def rms_inverse(hidden):
    return lax.rsqrt(jnp.mean(hidden * hidden, axis=-1, keepdims=True) + EPSILON)


def rms_grad(hidden, gain_vec, inv_rms, grad_out):
    normed = hidden * inv_rms
    grad_normed = grad_out * gain_vec
    return inv_rms * (grad_normed - normed * jnp.mean(grad_normed * normed, axis=-1, keepdims=True))


def expert_inner(slot_rows, gate_mat, up_mat):
    pre_gate = jnp.dot(slot_rows, gate_mat, preferred_element_type=jnp.float32)
    pre_up = jnp.dot(slot_rows, up_mat, preferred_element_type=jnp.float32)
    active = (jax.nn.silu(pre_gate) * pre_up).astype(jnp.bfloat16)
    return (pre_gate, pre_up, active)


def half_backward(slot_rows, slot_grads, pre_gate, pre_up, active, gate_mat, up_mat, down_mat):
    sigmoid_gate = jax.nn.sigmoid(pre_gate)
    silu_gate = pre_gate * sigmoid_gate
    grad_active = jnp.einsum("sd,fd->sf", slot_grads, down_mat, preferred_element_type=jnp.float32)
    grad_gate = (
        grad_active * pre_up * sigmoid_gate * (1.0 + pre_gate * (1.0 - sigmoid_gate))
    ).astype(jnp.bfloat16)
    grad_up = (grad_active * silu_gate).astype(jnp.bfloat16)
    input_part = jnp.einsum("sf,df->sd", grad_gate, gate_mat, preferred_element_type=jnp.float32)
    input_part = (
        input_part + jnp.einsum("sf,df->sd", grad_up, up_mat, preferred_element_type=jnp.float32)
    ).astype(jnp.bfloat16)
    gate_term = jnp.einsum("sd,sf->df", slot_rows, grad_gate, preferred_element_type=jnp.float32)
    up_term = jnp.einsum("sd,sf->df", slot_rows, grad_up, preferred_element_type=jnp.float32)
    down_term = jnp.einsum("sf,sd->fd", active, slot_grads, preferred_element_type=jnp.float32)
    return (input_part, gate_term, up_term, down_term)


def tensor_rows(source, weights):
    return lax.psum_scatter(
        jnp.dot(source, weights, preferred_element_type=jnp.float32),
        "tp",
        scatter_dimension=0,
        tiled=True,
    )


def group_rows(local_rows):
    return lax.all_gather(local_rows, "tp", axis=0, tiled=True)


def dispatch_rows(payload):
    return lax.all_to_all(payload, ("ctx", "tp"), split_axis=0, concat_axis=0, tiled=True)


def return_rows(payload):
    return lax.all_to_all(payload, ("ctx", "tp"), split_axis=0, concat_axis=0, tiled=True)


def pair_share(rows):
    return swapped(rows, "tp", 0)


def pair_add(keep_part, give_part):
    received = swapped(give_part, "tp", 0)
    return (keep_part.astype(jnp.float32) + received.astype(jnp.float32)).astype(jnp.bfloat16)


def local(
    attention,
    residual,
    w_out,
    w_qkv,
    norm_moe,
    norm_attn,
    expert_ids,
    expert_gates,
    w_gate,
    w_up,
    w_down,
    d_projected,
    d_stream,
):
    ctx_count = lax.axis_size("ctx")
    tensor_count = lax.axis_size("tp")
    local_tokens = attention.shape[0] // tensor_count
    model_width = residual.shape[1]
    device_count = ctx_count * tensor_count
    expert_count = device_count // 2
    top_count = expert_ids.shape[1]
    capacity = 2 * max(1, local_tokens * top_count * 3 // (4 * expert_count))
    half_cap = capacity // 2
    slot_count = device_count * half_cap
    hidden = residual.astype(jnp.float32) + tensor_rows(attention, w_out)
    inv_one = rms_inverse(hidden)
    moe_input = (hidden * inv_one * norm_moe).astype(jnp.bfloat16)
    flat_ids = expert_ids.reshape(-1)
    expert_range = jnp.arange(expert_count, dtype=jnp.int32)
    onehot = (flat_ids[:, None] == expert_range[None, :]).astype(jnp.int32)
    position = jnp.sum((jnp.cumsum(onehot, axis=0) - onehot) * onehot, axis=1)
    slot_index = flat_ids * capacity + position
    slot_range = jnp.arange(expert_count * capacity, dtype=jnp.int32)
    matches = slot_index.reshape(local_tokens, top_count)[None, :, :] == slot_range[:, None, None]
    select = jnp.any(matches, axis=2).astype(jnp.bfloat16)
    gate_map = jnp.sum(jnp.where(matches, expert_gates[None, :, :], 0.0), axis=2)
    send_rows = jnp.dot(select, moe_input, preferred_element_type=jnp.float32).astype(jnp.bfloat16)
    arrived = dispatch_rows(send_rows.reshape(device_count, half_cap, model_width)).reshape(
        slot_count, model_width
    )
    gate_mine = w_gate[0]
    up_mine = w_up[0]
    down_mine = w_down[0]
    rows_full = jnp.concatenate([arrived, pair_share(arrived)], axis=0)
    pre_gate, pre_up, active = expert_inner(rows_full, gate_mine, up_mine)
    partial_value = jnp.dot(active, down_mine, preferred_element_type=jnp.float32).astype(
        jnp.bfloat16
    )
    produced = pair_add(partial_value[:slot_count], partial_value[slot_count:])
    returned = return_rows(produced.reshape(device_count, half_cap, model_width)).reshape(
        expert_count * capacity, model_width
    )
    picked = returned[slot_index].reshape(local_tokens, top_count, model_width)
    moe_out = jnp.sum(picked.astype(jnp.float32) * expert_gates[:, :, None], axis=1)
    stream_sum = hidden + moe_out
    stream = stream_sum.astype(jnp.bfloat16)
    inv_two = rms_inverse(stream_sum)
    attn_input = (stream_sum * inv_two * norm_attn).astype(jnp.bfloat16)
    attn_rows = group_rows(attn_input)
    projected = jnp.einsum(
        "td,od->to", attn_rows, w_qkv, preferred_element_type=jnp.float32
    ).astype(jnp.bfloat16)
    grad_attn_in = tensor_rows(d_projected, w_qkv)
    grad_stream = d_stream.astype(jnp.float32) + rms_grad(
        stream_sum, norm_attn, inv_two, grad_attn_in
    )
    grad_slots = jnp.dot(
        gate_map, grad_stream, precision=lax.Precision.HIGHEST, preferred_element_type=jnp.float32
    )
    grad_slots = grad_slots.astype(jnp.bfloat16).reshape(device_count, half_cap, model_width)
    grad_arrived = dispatch_rows(grad_slots).reshape(slot_count, model_width)
    grads_full = jnp.concatenate([grad_arrived, pair_share(grad_arrived)], axis=0)
    part_full, gate_grad, up_grad, down_grad = half_backward(
        rows_full, grads_full, pre_gate, pre_up, active, gate_mine, up_mine, down_mine
    )
    grad_input = pair_add(part_full[:slot_count], part_full[slot_count:])
    back_rows = return_rows(grad_input.reshape(device_count, half_cap, model_width)).reshape(
        expert_count * capacity, model_width
    )
    grad_moe_in = jnp.sum(
        back_rows[slot_index].reshape(local_tokens, top_count, model_width).astype(jnp.float32),
        axis=1,
    )
    grad_hidden = grad_stream + rms_grad(hidden, norm_moe, inv_one, grad_moe_in)
    grad_residual = grad_hidden.astype(jnp.bfloat16)
    grad_rows_all = group_rows(grad_residual)
    grad_attention = jnp.einsum(
        "td,kd->tk", grad_rows_all, w_out, preferred_element_type=jnp.float32
    ).astype(jnp.bfloat16)
    out_partial = jnp.einsum(
        "tk,td->kd", attention, grad_rows_all, preferred_element_type=jnp.float32
    )
    out_weight_grad = lax.psum_scatter(out_partial, "ctx", scatter_dimension=1, tiled=True)
    return (
        projected,
        stream,
        grad_attention,
        grad_residual,
        out_weight_grad.astype(jnp.bfloat16),
        gate_grad.astype(jnp.bfloat16)[None],
        up_grad.astype(jnp.bfloat16)[None],
        down_grad.astype(jnp.bfloat16)[None],
    )


def solution(mesh):
    in_specs = (
        P("ctx", "tp"),
        P(("ctx", "tp"), None),
        P("tp", None),
        P("tp", None),
        P(),
        P(),
        P(("ctx", "tp"), None),
        P(("ctx", "tp"), None),
        P(("ctx", "tp"), None, None),
        P(("ctx", "tp"), None, None),
        P(("ctx", "tp"), None, None),
        P("ctx", "tp"),
        P(("ctx", "tp"), None),
    )
    out_specs = (
        P("ctx", "tp"),
        P(("ctx", "tp"), None),
        P("ctx", "tp"),
        P(("ctx", "tp"), None),
        P("tp", "ctx"),
        P(("ctx", "tp"), None, None),
        P(("ctx", "tp"), None, None),
        P(("ctx", "tp"), None, None),
    )
    return jax.shard_map(local, mesh=mesh, in_specs=in_specs, out_specs=out_specs, check_vma=False)
```

profile of v0, /device:TPU:0, one launch (start us, length us, event | category | flops | bytes accessed | tf_op | source)
XLA Modules:
  0.0 913.7 jit_solution(2600129608861352997)
XLA Ops:
  15.4 46.7 %reduce-scatter.4.cloned.1.call-done = f32[128,2048]{1,0:T(8,128)} async-done(((f32[512,2048]{1,0:T(8,128)}), f32[128,2048]{1,0:T(8,128)}) %reduce-scatter.4.cloned.1.call-update) | async-done | bytes 1048592 | tf_op jit(solution)/shard_map/reduce_scatter | solution.py:55
  67.8 6.2 reshape.127
  74.0 60.9 %all_to_all.20 = bf16[128,6,2048]{2,1,0:T(8,128)(2,1)} all-to-all(bf16[128,6,2048]{2,1,0:T(8,128)(2,1)} %reshape.127), channel_id=1, replica_groups=mesh['ctx'=32,'tp'=4] {'ctx','tp'}, dimensions={0} | all-to-all | bytes 6291456 | tf_op jit(solution)/shard_map/all_to_all | solution.py:68
  134.9 6.3 reshape.128
  149.5 96.0 %collective-permute-done = bf16[768,2048]{1,0:T(8,128)(2,1)} collective-permute-done((bf16[768,2048]{1,0:T(8,128)(2,1)}, bf16[768,2048]{1,0:T(8,128)(2,1)}, u32[]{:S(2)}, u32[]{:S(2)}) %collective-permute-start) | collective-permute-done | bytes 3145760 | tf_op jit(solution)/shard_map/ppermute | solution.py:16
  261.3 68.5 %collective-permute-done.1 = bf16[768,2048]{1,0:T(8,128)(2,1)S(1)} collective-permute-done((bf16[768,2048]{1,0:T(8,128)(2,1)S(1)}, bf16[768,2048]{1,0:T(8,128)(2,1)S(1)}, u32[]{:S(2)}, u32[]{:S(2)}) %collective-permute-start.1) | collective-permute-done | bytes 3145760 | tf_op jit(solution)/shard_map/ppermute | solution.py:16
  333.0 6.2 reshape.129
  347.3 50.0 %all-to-all-done.1 = bf16[128,6,2048]{2,1,0:T(8,128)(2,1)} async-done(((bf16[128,6,2048]{2,1,0:T(8,128)(2,1)}), bf16[128,6,2048]{2,1,0:T(8,128)(2,1)}, u32[]{:S(2)}, u32[]{:S(2)}) %all-to-all-start.1) | async-done | bytes 3145760 | tf_op jit(solution)/shard_map/all_to_all | solution.py:72
  397.3 6.3 reshape.130
  403.6 7.6 gather_fusion
  426.7 8.3 convolution_convert_fusion.1
  435.0 6.3 reshape.131
  441.2 58.1 %all_to_all.21 = bf16[128,6,2048]{2,1,0:T(8,128)(2,1)} all-to-all(bf16[128,6,2048]{2,1,0:T(8,128)(2,1)} %reshape.131), channel_id=1, replica_groups=mesh['ctx'=32,'tp'=4] {'ctx','tp'}, dimensions={0} | all-to-all | bytes 6291456 | tf_op jit(solution)/shard_map/all_to_all | solution.py:68
  499.4 6.3 reshape.132
  509.2 67.2 %collective-permute-done.2 = bf16[768,2048]{1,0:T(8,128)(2,1)S(1)} collective-permute-done((bf16[768,2048]{1,0:T(8,128)(2,1)}, bf16[768,2048]{1,0:T(8,128)(2,1)S(1)}, u32[]{:S(2)}, u32[]{:S(2)}) %collective-permute-start.2) | collective-permute-done | bytes 3145760 | tf_op jit(solution)/shard_map/ppermute | solution.py:16
  593.8 68.5 %collective-permute-done.3 = bf16[768,2048]{1,0:T(8,128)(2,1)S(1)} collective-permute-done((bf16[768,2048]{1,0:T(8,128)(2,1)S(1)}, bf16[768,2048]{1,0:T(8,128)(2,1)S(1)}, u32[]{:S(2)}, u32[]{:S(2)}) %collective-permute-start.3) | collective-permute-done | bytes 3145760 | tf_op jit(solution)/shard_map/ppermute | solution.py:16
  671.6 58.3 %all_to_all.22 = bf16[128,6,2048]{2,1,0:T(8,128)(2,1)} all-to-all(bf16[128,6,2048]{2,1,0:T(8,128)(2,1)} %reshape.133), channel_id=1, replica_groups=mesh['ctx'=32,'tp'=4] {'ctx','tp'}, dimensions={0} | all-to-all | bytes 6291456 | tf_op jit(solution)/shard_map/all_to_all | solution.py:72
  729.9 6.3 reshape.134
  736.2 7.5 gather_fusion.1
  760.9 25.9 %all-gather.5.cloned.1.call-done = bf16[512,2048]{1,0:T(8,128)(2,1)} async-done(((bf16[128,2048]{1,0:T(8,128)(2,1)}), bf16[512,2048]{1,0:T(8,128)(2,1)}) %all-gather.5.cloned.1.call-update) | async-done | bytes 2097168 | tf_op jit(solution)/shard_map/all_gather | solution.py:64
  791.8 7.1 fusion.2
  798.9 7.7 fusion.1
  813.2 6.6 all-gather.3.cloned.1.call-done
  824.1 81.3 %reduce-scatter.8.cloned.1.call-done = f32[512,64]{0,1:T(8,128)} async-done(((f32[512,2048]{0,1:T(8,128)}), f32[512,64]{0,1:T(8,128)}) %reduce-scatter.8.cloned.1.call-update) | async-done | bytes 131088 | tf_op jit(solution)/shard_map/reduce_scatter | solution.py:177
  (154 shorter events, 129.0 us)
Async XLA Ops:
  7.2 135.0 %copy-start = (bf16[768,2048]{1,0:T(8,128)(2,1)S(1)}, bf16[768,2048]{1,0:T(8,128)(2,1)}, u32[]{:S(2)}) copy-start(bf16[768,2048]{1,0:T(8,128)(2,1)} %param.16) | copy-start | bytes 9437188
  7.2 54.9 %reduce-scatter.4.cloned.1.call-start = ((), (), s32[]{:S(2)}) async-start(), calls=%async_computation.7 | async-start | bytes 5242880 | tf_op jit(solution)/shard_map/reduce_scatter | solution.py:55
  12.4 51.3 %copy-start.22 = (f32[2048]{0:T(1024)S(1)}, f32[2048]{0:T(1024)}, u32[]{:S(2)}) copy-start(f32[2048]{0:T(1024)} %param.17) | copy-start | bytes 24580
  12.4 411.8 %reduce-scatter.6.cloned.1.call-start = ((), (), s32[]{:S(2)}) async-start(), calls=%async_computation.9 | async-start | bytes 5242880 | tf_op jit(solution)/shard_map/reduce_scatter | solution.py:55
  141.2 104.3 %collective-permute-start = (bf16[768,2048]{1,0:T(8,128)(2,1)}, bf16[768,2048]{1,0:T(8,128)(2,1)}, u32[]{:S(2)}, u32[]{:S(2)}) collective-permute-start(bf16[768,2048]{1,0:T(8,128)(2,1)} %reshape.128), channel_id=1, source_target_pairs={{0,1},{1,0},{2,3},{3,2},{4,5},{5,4},{6,7},{7,6},{8,9},{9,8},{10,11... | collective-permute-start | bytes 9437192 | tf_op jit(solution)/shard_map/ppermute | solution.py:16
  149.5 98.3 %copy-start.12 = (bf16[1,2048,384]{2,1,0:T(8,128)(2,1)S(1)}, bf16[1,2048,384]{2,1,0:T(8,128)(2,1)}, u32[]{:S(2)}) copy-start(bf16[1,2048,384]{2,1,0:T(8,128)(2,1)} %param.21) | copy-start | bytes 4718596
  260.4 69.4 %collective-permute-start.1 = (bf16[768,2048]{1,0:T(8,128)(2,1)S(1)}, bf16[768,2048]{1,0:T(8,128)(2,1)S(1)}, u32[]{:S(2)}, u32[]{:S(2)}) collective-permute-start(bf16[768,2048]{1,0:T(8,128)(2,1)S(1)} %slice.30), channel_id=1, source_target_pairs={{0,1},{1,0},{2,3},{3,2},{4,5},{5,4},{6,7},{7,6},{8,9},{9,8},{10,11... | collective-permute-start | bytes 9437192 | tf_op jit(solution)/shard_map/ppermute | solution.py:16
  339.2 6.2 copy-start.26
  339.2 58.1 %all-to-all-start.1 = ((bf16[128,6,2048]{2,1,0:T(8,128)(2,1)}), bf16[128,6,2048]{2,1,0:T(8,128)(2,1)}, u32[]{:S(2)}, u32[]{:S(2)}) async-start(bf16[128,6,2048]{2,1,0:T(8,128)(2,1)} %reshape.129), calls=%async_computation.2 | async-start | bytes 8388608 | tf_op jit(solution)/shard_map/all_to_all | solution.py:72
  345.2 441.6 %all-gather.5.cloned.1.call-start = ((), (), s32[]{:S(2)}) async-start(), calls=%async_computation.10 | async-start | bytes 2621440 | tf_op jit(solution)/shard_map/all_gather | solution.py:64
  346.4 57.3 %copy-start.24 = (s32[1024]{0:T(1024)}, s32[1024]{0:T(1024)S(1)}, u32[]{:S(2)}) copy-start(s32[1024]{0:T(1024)S(1)} %pad_clamp_fusion) | copy-start | bytes 12292
  505.7 70.8 %collective-permute-start.2 = (bf16[768,2048]{1,0:T(8,128)(2,1)}, bf16[768,2048]{1,0:T(8,128)(2,1)S(1)}, u32[]{:S(2)}, u32[]{:S(2)}) collective-permute-start(bf16[768,2048]{1,0:T(8,128)(2,1)} %reshape.132), channel_id=1, source_target_pairs={{0,1},{1,0},{2,3},{3,2},{4,5},{5,4},{6,7},{7,6},{8,9},{9,8},{10,11... | collective-permute-start | bytes 9437192 | tf_op jit(solution)/shard_map/ppermute | solution.py:16
  509.2 67.6 %copy-start.34 = (bf16[1,384,2048]{2,1,0:T(8,128)(2,1)S(1)}, bf16[1,384,2048]{2,1,0:T(8,128)(2,1)}, u32[]{:S(2)}) copy-start(bf16[1,384,2048]{2,1,0:T(8,128)(2,1)} %param.23) | copy-start | bytes 4718596
  509.2 67.6 %copy-start.37 = (f32[1536,384]{1,0:T(8,128)S(1)}, f32[1536,384]{1,0:T(8,128)}, u32[]{:S(2)}) copy-start(f32[1536,384]{1,0:T(8,128)} %copy-done.36) | copy-start | bytes 7077892
  509.2 67.6 %copy-start.38 = (f32[1536,384]{1,0:T(8,128)S(1)}, f32[1536,384]{1,0:T(8,128)}, u32[]{:S(2)}) copy-start(f32[1536,384]{1,0:T(8,128)} %get-tuple-element.17) | copy-start | bytes 7077892
  590.4 71.8 %copy-start.6 = (bf16[1536,2048]{1,0:T(8,128)(2,1)S(1)}, bf16[1536,2048]{1,0:T(8,128)(2,1)}, u32[]{:S(2)}) copy-start(bf16[1536,2048]{1,0:T(8,128)(2,1)} %add_convert_fusion) | copy-start | bytes 18874372
  592.9 69.4 %collective-permute-start.3 = (bf16[768,2048]{1,0:T(8,128)(2,1)S(1)}, bf16[768,2048]{1,0:T(8,128)(2,1)S(1)}, u32[]{:S(2)}, u32[]{:S(2)}) collective-permute-start(bf16[768,2048]{1,0:T(8,128)(2,1)S(1)} %slice.32), channel_id=1, source_target_pairs={{0,1},{1,0},{2,3},{3,2},{4,5},{5,4},{6,7},{7,6},{8,9},{9,8},{10,11... | collective-permute-start | bytes 9437192 | tf_op jit(solution)/shard_map/ppermute | solution.py:16
  729.9 6.3 copy-start.25
  760.1 59.7 %all-gather.3.cloned.1.call-start = ((), (), s32[]{:S(2)}) async-start(), calls=%async_computation.8 | async-start | bytes 2621440 | tf_op jit(solution)/shard_map/all_gather | solution.py:64
  760.7 144.7 %reduce-scatter.8.cloned.1.call-start = ((), (), s32[]{:S(2)}) async-start(), calls=%async_computation.11 | async-start | bytes 4325376 | tf_op jit(solution)/shard_map/reduce_scatter | solution.py:177
  791.7 7.1 copy-start.21
  791.7 14.8 %slice-start = ((s8[6291456]{0:T(1024)(128)(4,1)}), s8[4194304]{0:T(1024)(128)(4,1)S(1)}, s32[]{:S(2)}) async-start(s8[6291456]{0:T(1024)(128)(4,1)} %bitcast.72), calls=%async_computation.12 | async-start | bytes 8388608
  798.8 7.7 slice-start.1
  798.8 7.7 copy-start.19
  (27 other events, 92.3 us)
Sparse Core Ops, SparseCore 0:
  12.5 49.5 reduce-scatter.3
  147.3 75.6 reduce-scatter.5
  760.2 26.5 all-gather.4
  788.9 30.8 all-gather.2
  823.3 82.0 reduce-scatter.7
where the time goes:
time: 920 us; the launch traced here: 914 us
  waiting for transfers between devices  511 us (56%)
  blocking collectives  177 us (19%)
  local copies, waits for them, and re-layouts  89 us (10%)
  matrix products  78.7 us (9%)
  other arithmetic  32.3 us (4%)
  between operations  14.5 us (2%)
  starting transfers between devices  10.6 us (1%)
    ppermute x4, waiting for transfers between devices, swapped(): return lax.ppermute(block, axis, route)  300 us
    all_to_all x2, blocking collectives, dispatch_rows(): lax.all_to_all(payload, ('ctx', 'tp'), split_axis=0, concat_axis=0, tiled...  119 us
    reduce_scatter x1, waiting for transfers between devices, local(): lax.psum_scatter(out_partial, 'ctx', scatter_dimension=1, tiled=True)  81.3 us
    all_to_all x1, blocking collectives, return_rows(): lax.all_to_all(payload, ('ctx', 'tp'), split_axis=0, concat_axis=0, tiled...  58.3 us
    all_to_all x1, waiting for transfers between devices, return_rows(): lax.all_to_all(payload, ('ctx', 'tp'), split_axis=0, concat_axis=0, tiled...  50 us
    reduce_scatter x2, waiting for transfers between devices, tensor_rows(): lax.psum_scatter(jnp.dot(source, weights, preferred_element_type=jnp.floa...  46.7 us
    all_gather x2, waiting for transfers between devices, group_rows(): return lax.all_gather(local_rows, 'tp', axis=0, tiled=True)  32.4 us
  transfers between devices with their start and end apart: 10, of which 9 were waited for; matrix products, arithmetic and copies ran while one was open for 10% of the time, Pallas kernels for 0%

commit v1 on v0

--- a/solution.py
+++ b/solution.py
@@ -61,7 +61,9 @@
 
 
 def group_rows(local_rows):
-    return lax.all_gather(local_rows, "tp", axis=0, tiled=True)
+    return jnp.concatenate(
+        lax.all_to_all(jnp.stack([local_rows] * lax.axis_size("tp")), "tp", 0, 0), axis=0
+    )
 
 
 def dispatch_rows(payload):

time: 920 us -> 887 us (0.964)
  waiting for transfers between devices: 511 us -> 439 us
  blocking collectives: 177 us -> 207 us
    reduce_scatter x1, waiting for transfers between devices: 81.3 us -> 34.1 us  [local(): lax.psum_scatter(out_partial, 'ctx', scatter_dimension=1, tiled=True)]
    all_gather x2 -> x0, waiting for transfers between devices: 32.4 us -> none  [group_rows(): return lax.all_gather(local_rows, 'tp', axis=0, tiled=True)]
    all_to_all x0 -> x1, blocking collectives: none -> 29.5 us  [group_rows(): lax.all_to_all(jnp.stack([local_rows] * lax.axis_size('tp')), 'tp', 0, 0)]
  transfers between devices with their start and end apart: 10 -> 9, of which waited for: 9 -> 8; matrix products, arithmetic and copies ran while one was open for 10% -> 11% of each run, Pallas kernels for 0% -> 0%
where the time goes in v1:
time: 887 us; the launch traced here: 880 us
  waiting for transfers between devices  439 us (49%)
  blocking collectives  207 us (23%)
  local copies, waits for them, and re-layouts  92.1 us (10%)
  matrix products  80.4 us (9%)
  other arithmetic  32.1 us (4%)
  starting transfers between devices  15 us (2%)
  between operations  14.7 us (2%)
    ppermute x4, waiting for transfers between devices, swapped(): return lax.ppermute(block, axis, route)  300 us
    all_to_all x2, blocking collectives, dispatch_rows(): lax.all_to_all(payload, ('ctx', 'tp'), split_axis=0, concat_axis=0, tiled...  119 us
    all_to_all x1, blocking collectives, return_rows(): lax.all_to_all(payload, ('ctx', 'tp'), split_axis=0, concat_axis=0, tiled...  58.4 us
    all_to_all x1, waiting for transfers between devices, return_rows(): lax.all_to_all(payload, ('ctx', 'tp'), split_axis=0, concat_axis=0, tiled...  49.8 us
    reduce_scatter x2, waiting for transfers between devices, tensor_rows(): lax.psum_scatter(jnp.dot(source, weights, preferred_element_type=jnp.floa...  46.7 us
    reduce_scatter x1, waiting for transfers between devices, local(): lax.psum_scatter(out_partial, 'ctx', scatter_dimension=1, tiled=True)  34.1 us
    all_to_all x1, blocking collectives, group_rows(): lax.all_to_all(jnp.stack([local_rows] * lax.axis_size('tp')), 'tp', 0, 0)  29.5 us
  transfers between devices with their start and end apart: 9, of which 8 were waited for; matrix products, arithmetic and copies ran while one was open for 11% of the time, Pallas kernels for 0%

profile of v1, /device:TPU:0, one launch (start us, length us, event | category | flops | bytes accessed | tf_op | source)
XLA Modules:
  0.0 880.4 jit_solution(4808245127993687649)
XLA Ops:
  15.4 46.7 %reduce-scatter.4.cloned.1.call-done = f32[128,2048]{1,0:T(8,128)} async-done(((f32[512,2048]{1,0:T(8,128)}), f32[128,2048]{1,0:T(8,128)}) %reduce-scatter.4.cloned.1.call-update) | async-done | bytes 1048592 | tf_op jit(solution)/shard_map/reduce_scatter | solution.py:55
  74.0 60.9 %all_to_all.30 = bf16[128,6,2048]{2,1,0:T(8,128)(2,1)} all-to-all(bf16[128,6,2048]{2,1,0:T(8,128)(2,1)} %reshape.137), channel_id=1, replica_groups=mesh['ctx'=32,'tp'=4] {'ctx','tp'}, dimensions={0} | all-to-all | bytes 6291456 | tf_op jit(solution)/shard_map/all_to_all | solution.py:70
  134.9 6.3 reshape.138
  149.5 96.0 %collective-permute-done = bf16[768,2048]{1,0:T(8,128)(2,1)} collective-permute-done((bf16[768,2048]{1,0:T(8,128)(2,1)}, bf16[768,2048]{1,0:T(8,128)(2,1)}, u32[]{:S(2)}, u32[]{:S(2)}) %collective-permute-start) | collective-permute-done | bytes 3145760 | tf_op jit(solution)/shard_map/ppermute | solution.py:16
  261.3 68.5 %collective-permute-done.1 = bf16[768,2048]{1,0:T(8,128)(2,1)S(1)} collective-permute-done((bf16[768,2048]{1,0:T(8,128)(2,1)S(1)}, bf16[768,2048]{1,0:T(8,128)(2,1)S(1)}, u32[]{:S(2)}, u32[]{:S(2)}) %collective-permute-start.1) | collective-permute-done | bytes 3145760 | tf_op jit(solution)/shard_map/ppermute | solution.py:16
  333.0 6.3 reshape.139
  347.5 49.8 %all-to-all-done.1 = bf16[128,6,2048]{2,1,0:T(8,128)(2,1)} async-done(((bf16[128,6,2048]{2,1,0:T(8,128)(2,1)}), bf16[128,6,2048]{2,1,0:T(8,128)(2,1)}, u32[]{:S(2)}, u32[]{:S(2)}) %all-to-all-start.1) | async-done | bytes 3145760 | tf_op jit(solution)/shard_map/all_to_all | solution.py:74
  397.3 6.3 reshape.140
  403.7 7.6 gather_fusion
  426.7 8.3 convolution_convert_fusion.1
  434.9 6.2 reshape.142
  441.2 58.1 %all_to_all.31 = bf16[128,6,2048]{2,1,0:T(8,128)(2,1)} all-to-all(bf16[128,6,2048]{2,1,0:T(8,128)(2,1)} %reshape.142), channel_id=1, replica_groups=mesh['ctx'=32,'tp'=4] {'ctx','tp'}, dimensions={0} | all-to-all | bytes 6291456 | tf_op jit(solution)/shard_map/all_to_all | solution.py:70
  499.3 6.3 reshape.143
  508.9 67.2 %collective-permute-done.2 = bf16[768,2048]{1,0:T(8,128)(2,1)S(1)} collective-permute-done((bf16[768,2048]{1,0:T(8,128)(2,1)}, bf16[768,2048]{1,0:T(8,128)(2,1)S(1)}, u32[]{:S(2)}, u32[]{:S(2)}) %collective-permute-start.2) | collective-permute-done | bytes 3145760 | tf_op jit(solution)/shard_map/ppermute | solution.py:16
  593.5 68.5 %collective-permute-done.3 = bf16[768,2048]{1,0:T(8,128)(2,1)S(1)} collective-permute-done((bf16[768,2048]{1,0:T(8,128)(2,1)S(1)}, bf16[768,2048]{1,0:T(8,128)(2,1)S(1)}, u32[]{:S(2)}, u32[]{:S(2)}) %collective-permute-start.3) | collective-permute-done | bytes 3145760 | tf_op jit(solution)/shard_map/ppermute | solution.py:16
  671.2 58.4 %all_to_all.32 = bf16[128,6,2048]{2,1,0:T(8,128)(2,1)} all-to-all(bf16[128,6,2048]{2,1,0:T(8,128)(2,1)} %reshape.144), channel_id=1, replica_groups=mesh['ctx'=32,'tp'=4] {'ctx','tp'}, dimensions={0} | all-to-all | bytes 6291456 | tf_op jit(solution)/shard_map/all_to_all | solution.py:74
  729.6 6.3 reshape.145
  735.9 7.5 gather_fusion.1
  759.8 29.5 %all_to_all.33 = bf16[4,128,2048]{2,1,0:T(8,128)(2,1)S(1)} all-to-all(bf16[4,128,2048]{2,1,0:T(8,128)(2,1)S(1)} %stack.5), channel_id=1, replica_groups=mesh['ctx'=32,'tp'=4] {'tp'}, dimensions={0} | all-to-all | bytes 4194304 | tf_op jit(solution)/shard_map/all_to_all | solution.py:65
  794.0 7.0 fusion.2
  807.4 8.0 fusion.1
  815.4 7.7 fusion
  825.2 8.3 all-to-all-done.2
  837.8 34.1 %reduce-scatter.8.cloned.1.call-done = f32[512,64]{0,1:T(8,128)} async-done(((f32[512,2048]{0,1:T(8,128)}), f32[512,64]{0,1:T(8,128)}) %reduce-scatter.8.cloned.1.call-update) | async-done | bytes 131088 | tf_op jit(solution)/shard_map/reduce_scatter | solution.py:179
  (154 shorter events, 135.8 us)
Async XLA Ops:
  7.2 135.1 %copy-start = (bf16[768,2048]{1,0:T(8,128)(2,1)S(1)}, bf16[768,2048]{1,0:T(8,128)(2,1)}, u32[]{:S(2)}) copy-start(bf16[768,2048]{1,0:T(8,128)(2,1)} %param.16) | copy-start | bytes 9437188
  7.2 54.9 %reduce-scatter.4.cloned.1.call-start = ((), (), s32[]{:S(2)}) async-start(), calls=%async_computation.9 | async-start | bytes 5242880 | tf_op jit(solution)/shard_map/reduce_scatter | solution.py:55
  12.4 51.3 %copy-start.25 = (f32[2048]{0:T(1024)S(1)}, f32[2048]{0:T(1024)}, u32[]{:S(2)}) copy-start(f32[2048]{0:T(1024)} %param.17) | copy-start | bytes 24580
  12.4 411.8 %reduce-scatter.6.cloned.1.call-start = ((), (), s32[]{:S(2)}) async-start(), calls=%async_computation.10 | async-start | bytes 5242880 | tf_op jit(solution)/shard_map/reduce_scatter | solution.py:55
  141.2 104.4 %collective-permute-start = (bf16[768,2048]{1,0:T(8,128)(2,1)}, bf16[768,2048]{1,0:T(8,128)(2,1)}, u32[]{:S(2)}, u32[]{:S(2)}) collective-permute-start(bf16[768,2048]{1,0:T(8,128)(2,1)} %reshape.138), channel_id=1, source_target_pairs={{0,1},{1,0},{2,3},{3,2},{4,5},{5,4},{6,7},{7,6},{8,9},{9,8},{10,11... | collective-permute-start | bytes 9437192 | tf_op jit(solution)/shard_map/ppermute | solution.py:16
  149.5 98.4 %copy-start.16 = (bf16[1,2048,384]{2,1,0:T(8,128)(2,1)S(1)}, bf16[1,2048,384]{2,1,0:T(8,128)(2,1)}, u32[]{:S(2)}) copy-start(bf16[1,2048,384]{2,1,0:T(8,128)(2,1)} %param.21) | copy-start | bytes 4718596
  260.4 69.4 %collective-permute-start.1 = (bf16[768,2048]{1,0:T(8,128)(2,1)S(1)}, bf16[768,2048]{1,0:T(8,128)(2,1)S(1)}, u32[]{:S(2)}, u32[]{:S(2)}) collective-permute-start(bf16[768,2048]{1,0:T(8,128)(2,1)S(1)} %slice.30), channel_id=1, source_target_pairs={{0,1},{1,0},{2,3},{3,2},{4,5},{5,4},{6,7},{7,6},{8,9},{9,8},{10,11... | collective-permute-start | bytes 9437192 | tf_op jit(solution)/shard_map/ppermute | solution.py:16
  339.3 6.4 copy-start.29
  339.3 58.0 %all-to-all-start.1 = ((bf16[128,6,2048]{2,1,0:T(8,128)(2,1)}), bf16[128,6,2048]{2,1,0:T(8,128)(2,1)}, u32[]{:S(2)}, u32[]{:S(2)}) async-start(bf16[128,6,2048]{2,1,0:T(8,128)(2,1)} %reshape.139), calls=%async_computation.2 | async-start | bytes 8388608 | tf_op jit(solution)/shard_map/all_to_all | solution.py:74
  345.2 526.7 %reduce-scatter.8.cloned.1.call-start = ((), (), s32[]{:S(2)}) async-start(), calls=%async_computation.11 | async-start | bytes 4325376 | tf_op jit(solution)/shard_map/reduce_scatter | solution.py:179
  346.6 57.1 %copy-start.27 = (s32[1024]{0:T(1024)}, s32[1024]{0:T(1024)S(1)}, u32[]{:S(2)}) copy-start(s32[1024]{0:T(1024)S(1)} %pad_clamp_fusion) | copy-start | bytes 12292
  505.6 70.5 %collective-permute-start.2 = (bf16[768,2048]{1,0:T(8,128)(2,1)}, bf16[768,2048]{1,0:T(8,128)(2,1)S(1)}, u32[]{:S(2)}, u32[]{:S(2)}) collective-permute-start(bf16[768,2048]{1,0:T(8,128)(2,1)} %reshape.143), channel_id=1, source_target_pairs={{0,1},{1,0},{2,3},{3,2},{4,5},{5,4},{6,7},{7,6},{8,9},{9,8},{10,11... | collective-permute-start | bytes 9437192 | tf_op jit(solution)/shard_map/ppermute | solution.py:16
  508.9 67.6 %copy-start.37 = (bf16[1,384,2048]{2,1,0:T(8,128)(2,1)S(1)}, bf16[1,384,2048]{2,1,0:T(8,128)(2,1)}, u32[]{:S(2)}) copy-start(bf16[1,384,2048]{2,1,0:T(8,128)(2,1)} %param.23) | copy-start | bytes 4718596
  508.9 67.6 %copy-start.40 = (f32[1536,384]{1,0:T(8,128)S(1)}, f32[1536,384]{1,0:T(8,128)}, u32[]{:S(2)}) copy-start(f32[1536,384]{1,0:T(8,128)} %copy-done.39) | copy-start | bytes 7077892
  508.9 67.6 %copy-start.41 = (f32[1536,384]{1,0:T(8,128)S(1)}, f32[1536,384]{1,0:T(8,128)}, u32[]{:S(2)}) copy-start(f32[1536,384]{1,0:T(8,128)} %get-tuple-element.17) | copy-start | bytes 7077892
  590.1 71.9 %copy-start.6 = (bf16[1536,2048]{1,0:T(8,128)(2,1)S(1)}, bf16[1536,2048]{1,0:T(8,128)(2,1)}, u32[]{:S(2)}) copy-start(bf16[1536,2048]{1,0:T(8,128)(2,1)} %add_convert_fusion) | copy-start | bytes 18874372
  592.5 69.4 %collective-permute-start.3 = (bf16[768,2048]{1,0:T(8,128)(2,1)S(1)}, bf16[768,2048]{1,0:T(8,128)(2,1)S(1)}, u32[]{:S(2)}, u32[]{:S(2)}) collective-permute-start(bf16[768,2048]{1,0:T(8,128)(2,1)S(1)} %slice.32), channel_id=1, source_target_pairs={{0,1},{1,0},{2,3},{3,2},{4,5},{5,4},{6,7},{7,6},{8,9},{9,8},{10,11... | collective-permute-start | bytes 9437192 | tf_op jit(solution)/shard_map/ppermute | solution.py:16
  759.5 29.8 %copy-start.12 = (bf16[128,2048]{1,0:T(8,128)(2,1)}, bf16[128,2048]{1,0:T(8,128)(2,1)S(1)}, u32[]{:S(2)}) copy-start(bf16[128,2048]{1,0:T(8,128)(2,1)S(1)} %get-tuple-element.12) | copy-start | bytes 1572868
  759.8 30.9 %copy-start.15 = (bf16[512,512]{1,0:T(8,128)(2,1)S(1)}, bf16[512,512]{1,0:T(8,128)(2,1)}, u32[]{:S(2)}) copy-start(bf16[512,512]{1,0:T(8,128)(2,1)} %param.13) | copy-start | bytes 1572868
  793.9 7.0 copy-start.13
  802.6 30.9 %all-to-all-start.2 = ((bf16[4,128,2048]{2,1,0:T(8,128)(2,1)}), bf16[4,128,2048]{2,1,0:T(8,128)(2,1)}, u32[]{:S(2)}, u32[]{:S(2)}) async-start(bf16[4,128,2048]{2,1,0:T(8,128)(2,1)} %stack.4), calls=%async_computation.3 | async-start | bytes 4194304 | tf_op jit(solution)/shard_map/all_to_all | solution.py:65
  807.3 8.0 copy-start.23
  815.4 7.8 copy-start.10
  815.4 7.8 copy-start.14
  (27 other events, 90.8 us)
Sparse Core Ops, SparseCore 0:
  12.5 49.5 reduce-scatter.3
  147.4 75.6 reduce-scatter.5
  794.1 77.8 reduce-scatter.7
